TPU v7x, 32 devices: a whole 2x2x4 slice. The times are simulated.
32 devices in a mesh: rows: 8 (over z, y), scen: 4 (over x, core).
Axes of the slice: x: 2, y: 2, z: 4, core: 2. Of those that a mesh axis runs over, the one named last changes fastest.
Arguments:
- inverse: bfloat16 [4096, 16384], P('scen', 'rows'), as said below
- voltage_prev: float32 [64, 16384], P('scen', 'rows'), may hold values from -6 to 6
- line_delay: int32 [8, 16], P('rows'), may hold values from 0 to 4, as said below
- line_bus: int32 [8, 16], P('rows'), may hold values from 0 to 2047
- line_impedance: float32 [8, 16], P('rows'), may hold values from 0.5 to 2, as said below
- line_past: float32 [4, 2, 64, 8, 16], P(None, None, 'scen', 'rows'), may hold values from -6 to 6
- model_dest: int32 [1024, 1], P('rows'), may hold values from 0 to 7; in each aligned block of 128 rows (0 to 127, 128 to 255, ...) at most 32 rows name the same one
- model_bus: int32 [1024], P('rows'), may hold values from 0 to 2047
- model_gain: float32 [1024], P('rows'), may hold values from 0.3 to 3
- model_lag: float32 [1024], P('rows'), may hold values from 0.1 to 0.9
- model_state: float32 [64, 1024], P('scen', 'rows'), may hold values from -6 to 6
- model_source: float32 [6, 64, 1024], P(None, 'scen', 'rows'), may hold values from -6 to 6
- switch_bus: int32 [2, 64, 4], P(None, 'scen'), may hold values from 0 to 4095, as said below
- switch_admittance: float32 [64, 4], P('scen'), may hold values from 0.5 to 4
Outputs:
- voltage: float32 [64, 16384], P('scen', 'rows')
- model_current: float32 [64, 1024], P('scen', 'rows')
Inputs may be any that keep to these rules, and one draw needn't show every extreme that they name: `line_delay`: A line joins end (p, q * 2 + c) with end (q, p * 2 + c), with the same delay and impedance at both ends; no line joins the two devices of one subnetwork; delays of lines run from 2 to 4. `line_impedance`: equal at both ends of a line. `switch_bus`: the two buses of a switched branch differ. `inverse`: each block of 4096 columns is symmetric. `model_dest`: among the models of one index of rows at most 32 name the same index.
All inputs are finite; a program needn't handle non-finite values.
Results may differ from a plain program's by a relative error of at most 0.0024.
The roundings to bfloat16 on the way count: a program that leaves them out, or rounds other values in their place, can miss the bound.
Values may be sent and summed in bfloat16 or wider, within the bound.
A program may use at most 128 MiB of HBM per device.

v0:
```python
import jax
import jax.numpy as jnp
from jax import lax
from jax.sharding import PartitionSpec as P


def swapped(value, axis, apart):
    mask = 2**apart
    pairs = [(source, source ^ mask) for source in range(lax.axis_size(axis))]
    return lax.ppermute(value, axis, pairs)


def slot_table(targets, sections, slots):
    onehot = (targets[:, None] == jnp.arange(sections, dtype=jnp.int32)[None, :]).astype(jnp.int32)
    count = targets.shape[0]
    earlier = (
        jnp.arange(count, dtype=jnp.int32)[None, :] < jnp.arange(count, dtype=jnp.int32)[:, None]
    )
    same = targets[:, None] == targets[None, :]
    rank = jnp.sum((earlier & same).astype(jnp.int32), axis=1)
    return targets * slots + rank


def exact_dot(left, right):
    return jnp.dot(left, right, precision=lax.Precision.HIGHEST)


def per_device(
    inverse,
    voltage_prev,
    line_delay,
    line_bus,
    line_impedance,
    line_past,
    model_dest,
    model_bus,
    model_gain,
    model_lag,
    model_state,
    model_source,
    switch_bus,
    switch_admittance,
):
    n = lax.axis_size("rows")
    groups = lax.axis_size("scen")
    place = lax.axis_index("rows")
    share = lax.axis_index("scen")
    subnet = place // 2
    half = place % 2
    lower = half == 0
    depth_rows, width = inverse.shape
    scen = voltage_prev.shape[0]
    steps = model_source.shape[0]
    ends = line_bus.shape[1]
    models = model_bus.shape[0]
    depth_max = line_past.shape[0]
    slots = max(2, 2 * models // n)
    cap = n * slots
    f32, bf16 = (jnp.float32, jnp.bfloat16)

    def by_half(own, other):
        return jnp.where(
            lower, jnp.concatenate([own, other], -1), jnp.concatenate([other, own], -1)
        )

    slot = slot_table(model_dest[:, 0], n, slots)
    placing = (slot[:, None] == jnp.arange(cap, dtype=jnp.int32)[None, :]).astype(f32)
    bus_out = exact_dot((model_bus + 1).astype(f32)[None], placing)
    bus_out = jnp.broadcast_to(
        bus_out.reshape(n // 2, 1, 2 * slots), (n // 2, 2, 2 * slots)
    ).reshape(n, 2 * slots)
    ends_out = jnp.broadcast_to(line_bus.astype(f32) + 1.0, (n, ends))
    buses = lax.all_to_all(jnp.concatenate([bus_out, ends_out], 1), "rows", 0, 0, tiled=True)
    model_pts = buses[:, : 2 * slots].reshape(n, 2, slots).transpose(1, 0, 2).reshape(2, cap)
    ends_pts = lax.dynamic_slice_in_dim(buses[:, 2 * slots :], subnet * 2, 2, axis=0)
    half_pts = jnp.concatenate([model_pts, ends_pts], 1).astype(jnp.int32) - 1
    pts = jnp.where(half_pts < 0, -1, half_pts + jnp.array([[0], [width]], jnp.int32)).reshape(-1)
    own_pts = lax.dynamic_index_in_dim(half_pts, half, 0, keepdims=False)
    hp = cap + ends
    payload = jnp.concatenate(
        [
            model_lag[None],
            ((1.0 - model_lag) * model_gain)[None],
            model_state,
            model_source.reshape(steps * scen, models),
        ],
        0,
    )
    sent = exact_dot(payload, placing).reshape(-1, n // 2, 1, 2 * slots)
    sent = (
        jnp.broadcast_to(sent, (payload.shape[0], n // 2, 2, 2 * slots))
        .reshape(-1, n, 2 * slots)
        .transpose(1, 0, 2)
    )
    got = lax.all_to_all(sent, "rows", 0, 0, tiled=True)
    got = got.reshape(n, -1, 2, slots).transpose(1, 2, 0, 3).reshape(-1, 2, cap)
    zeros_ends = jnp.zeros((got.shape[0], 2, ends), f32)
    got = jnp.concatenate([got, zeros_ends], 2).reshape(-1, 2 * hp)
    lag, gain, current = (got[0], got[1], got[2 : 2 + scen])
    source = got[2 + scen :].reshape(steps, scen, 2 * hp)
    col_sel = (jnp.arange(width, dtype=jnp.int32)[:, None] == own_pts[None, :]).astype(bf16)
    first_all = lax.dynamic_index_in_dim(
        lax.all_gather(switch_bus[0], "scen", axis=0, tiled=True), subnet, 1, keepdims=False
    )
    second_all = lax.dynamic_index_in_dim(
        lax.all_gather(switch_bus[1], "scen", axis=0, tiled=True), subnet, 1, keepdims=False
    )
    row_ids = jnp.arange(depth_rows, dtype=jnp.int32)[None, :] + share * depth_rows
    col_ids = jnp.arange(width, dtype=jnp.int32)[None, :] + half * width
    picks = (row_ids == first_all[:, None]).astype(bf16) - (row_ids == second_all[:, None]).astype(
        bf16
    )
    col_picks = (col_ids == first_all[:, None]).astype(f32) - (
        col_ids == second_all[:, None]
    ).astype(f32)
    row_sel = (row_ids == pts[:, None]).astype(bf16)
    narrow = jnp.dot(inverse, col_sel, preferred_element_type=f32).astype(bf16)
    part = jnp.dot(row_sel, narrow, preferred_element_type=f32).astype(bf16)
    own_cols = lax.psum(part, "scen")
    branch_part = jnp.dot(picks, inverse, preferred_element_type=f32)
    pts_part = jnp.dot(picks, narrow, preferred_element_type=f32)
    depth_part = jnp.sum(branch_part * col_picks, axis=1, keepdims=True)
    side = lax.psum(jnp.concatenate([pts_part, depth_part], 1), "scen")
    side = lax.dynamic_slice_in_dim(side, share * scen, scen, axis=0)
    own_diag = lax.dynamic_slice_in_dim(own_cols, half * hp, hp, axis=0)
    cross = lax.dynamic_slice_in_dim(own_cols, (1 - half) * hp, hp, axis=0).T
    other_diag = swapped(own_diag, "rows", 0)
    other_cols = jnp.where(
        lower, jnp.concatenate([cross, other_diag], 0), jnp.concatenate([other_diag, cross], 0)
    )
    matrix = by_half(own_cols, other_cols)
    volt0 = exact_dot(voltage_prev, col_sel.astype(f32))
    past = line_past[:, :, :, 0, :].reshape(depth_max * 2 * scen, ends)
    line_info = jnp.concatenate([past, line_delay.astype(f32), line_impedance], 0)
    other_side = swapped(side, "rows", 0)
    other_volt = swapped(volt0, "rows", 0)
    other_info = swapped(line_info, "rows", 0)
    depth = (side + other_side)[:, hp]
    branch = by_half(side[:, :hp], other_side[:, :hp])
    volt = by_half(volt0, other_volt)
    info = jnp.stack([line_info, other_info])
    info = jnp.where(lower, info, info[::-1])
    past = info[:, : depth_max * 2 * scen].reshape(2, depth_max, 2, scen, ends)
    history = [past[:, k] for k in range(depth_max)]
    delays = info[:, -2][:, None, :]
    impedance = info[:, -1][:, None, :]
    admit = lax.dynamic_index_in_dim(switch_admittance, subnet, axis=1, keepdims=False)
    same = pts[:, None] == pts[None, :]
    before = (
        jnp.arange(2 * hp, dtype=jnp.int32)[:, None] < jnp.arange(2 * hp, dtype=jnp.int32)[None, :]
    )
    leading = jnp.sum((same & before).astype(jnp.int32), axis=0) == 0
    merge = (same & leading[None, :]).astype(f32)
    for step in range(steps):
        current = lag * current + gain * (source[step] - volt)
        line_term = jnp.zeros((2, scen, ends), f32)
        for delay in range(2, depth_max + 1):
            older = history[step - delay + depth_max]
            line_term = line_term + jnp.where(
                delays == delay, -(2.0 / impedance) * older[:, 0] - older[:, 1], 0.0
            )
        zeros = jnp.zeros((scen, cap), f32)
        lines = jnp.concatenate([zeros, line_term[0], zeros, line_term[1]], 1)
        rhs = exact_dot(current - lines, merge).astype(bf16)
        along = jnp.sum(rhs.astype(f32) * branch, axis=1)
        factor = admit * along / (1.0 + admit * depth)
        if step + 1 < steps:
            base = jnp.dot(rhs, matrix, preferred_element_type=f32)
            volt = base - factor[:, None] * branch
        if step + 2 < steps:
            own_volt = jnp.where(lower, volt[:, cap:hp], volt[:, hp + cap :])
            own_term = jnp.where(lower, line_term[0], line_term[1])
            out = jnp.stack([own_volt, own_term]).reshape(2, scen, n // 2, 2 * ends // n)
            out = jnp.broadcast_to(
                out.transpose(2, 0, 1, 3)[:, None], (n // 2, 2, 2, scen, 2 * ends // n)
            )
            back = lax.all_to_all(out.reshape(n, 2, scen, 2 * ends // n), "rows", 0, 0, tiled=True)
            back = back.reshape(n, 2, scen, 2, ends // n).transpose(3, 1, 2, 0, 4)
            history.append(back.reshape(2, 2, scen, ends))
    rhs_all = lax.all_gather(rhs, "scen", axis=0, tiled=True)
    factor_all = lax.all_gather(factor[:, None], "scen", axis=0, tiled=True)
    dense = jnp.dot(rhs_all, row_sel, preferred_element_type=f32).astype(bf16)
    partial = jnp.dot(dense, inverse, preferred_element_type=f32) - factor_all * branch_part
    voltage = lax.psum_scatter(partial, "scen", scatter_dimension=0, tiled=True)
    own_current = jnp.where(lower, current[:, :cap], current[:, hp : hp + cap])
    back = lax.all_to_all(
        own_current.reshape(scen, n, slots).transpose(1, 0, 2), "rows", 0, 0, tiled=True
    )
    model_current = lax.dot_general(
        back.transpose(1, 0, 2).reshape(scen, cap),
        placing,
        (((1,), (1,)), ((), ())),
        precision=lax.Precision.HIGHEST,
    )
    return (voltage, model_current)


def solution(mesh):
    placed = (
        P("scen", "rows"),
        P("scen", "rows"),
        P("rows", None),
        P("rows", None),
        P("rows", None),
        P(None, None, "scen", "rows", None),
        P("rows", None),
        P("rows"),
        P("rows"),
        P("rows"),
        P("scen", "rows"),
        P(None, "scen", "rows"),
        P(None, "scen", None),
        P("scen", None),
    )
    return jax.shard_map(
        per_device,
        mesh=mesh,
        in_specs=placed,
        out_specs=(P("scen", "rows"), P("scen", "rows")),
        check_vma=False,
    )
```

profile of v0, /device:TPU:0, one launch (start us, length us, event | category | flops | bytes accessed | tf_op | source)
XLA Modules:
  0.0 226.6 jit_solution(2382398934178793982)
XLA Ops:
  11.1 7.3 %all-to-all-start.1 = ((f32[8,1,80]{2,1,0:T(1,128)}), f32[8,1,80]{2,1,0:T(1,128)S(1)}, u32[]{:S(2)}, u32[]{:S(2)}) async-start(f32[8,1,80]{2,1,0:T(1,128)} %bitcast.19), calls=%async_computation.1 | async-start | bytes 8192 | tf_op jit(solution)/shard_map/all_to_all | solution.py:73
  20.8 2.0 collective-permute-start.1
  23.7 5.2 %all-gather.1 = s32[1,64,4]{2,0,1:T(1,128)S(1)} all-gather(s32[1,16,4]{2,0,1:T(1,128)S(1)} %copy.320), channel_id=3, replica_groups=mesh['rows'=8,'scen'=4] {'scen'}, dimensions={1}, use_global_device_ids=true | all-gather | bytes 1280 | tf_op jit(solution)/shard_map/all_gather | solution.py:106
  29.0 5.2 %all-gather = s32[1,64,4]{2,0,1:T(1,128)S(1)} all-gather(s32[1,16,4]{2,0,1:T(1,128)S(1)} %copy.319), channel_id=2, replica_groups=mesh['rows'=8,'scen'=4] {'scen'}, dimensions={1}, use_global_device_ids=true | all-gather | bytes 1280 | tf_op jit(solution)/shard_map/all_gather | solution.py:103
  34.2 1.3 dynamic-slice_reduce_fusion
  35.5 1.3 dynamic-slice_reduce_fusion.1
  37.5 1.2 fusion.66
  38.7 3.2 %multiply_reduce_fusion = (f32[64]{0:T(128)S(1)}, f32[64,2048]{1,0:T(8,128)S(1)}) fusion(s32[2048]{0:T(1024)S(1)} %iota_add_fusion, s32[64]{0:T(128)S(1)} %dynamic-slice_reduce_fusion, s32[64]{0:T(128)S(1)} %dynamic-slice_reduce_fusion.1, bf16[1024,2048]{1,0:T(8,128)(2,1)} %param.15, s32[1024]{0:T(1024)S(1)} %iota_add_fusion.1), kind=kOutput, calls=%fused_computation.54 | convolution fusion | flops 269680576 | bytes 4731648 | tf_op jit(solution)/shard_map/dot_general | solution.py:120
  44.8 4.5 %all-to-all-start = ((f32[8,114,64]{1,2,0:T(8,128)}), f32[8,114,64]{1,2,0:T(8,128)S(1)}, u32[]{:S(2)}, u32[]{:S(2)}) async-start(f32[8,114,64]{1,2,0:T(8,128)} %bitcast.8), calls=%async_computation | async-start | bytes 524288 | tf_op jit(solution)/shard_map/all_to_all | solution.py:95
  49.7 4.1 %fusion.16 = bf16[272,1024]{1,0:T(8,128)(2,1)S(1)} fusion(bf16[1024,2048]{1,0:T(8,128)(2,1)} %param.15, s32[272]{0:T(512)S(1)} %fusion.142), kind=kOutput, calls=%fused_computation.21 | convolution fusion | flops 1142243328 | bytes 4752448 | tf_op jit(solution)/shard_map/dot_general | solution.py:117
  54.4 1.5 fusion.19
  57.7 2.0 collective-permute-start
  62.9 27.9 %all-reduce.5.cloned.1.call-done = bf16[544,272]{0,1:T(8,128)(2,1)} async-done(((bf16[544,272]{0,1:T(8,128)(2,1)}), bf16[544,272]{0,1:T(8,128)(2,1)}) %all-reduce.5.cloned.1.call-update) | async-done | bytes 295952 | tf_op jit(solution)/shard_map/psum | solution.py:119
  90.7 1.3 constant_dynamic-slice_fusion.4
  92.0 1.5 collective-permute-start.2
  93.6 31.6 %all-reduce.7.cloned.1.call-done = f32[64,273]{1,0:T(8,128)} async-done(((f32[64,273]{1,0:T(8,128)}), f32[64,273]{1,0:T(8,128)}) %all-reduce.7.cloned.1.call-update) | async-done | bytes 69904 | tf_op jit(solution)/shard_map/psum | solution.py:123
  125.9 1.5 collective-permute-start.3
  128.8 1.2 pad_slice_fusion.1
  131.9 1.6 multiply_reduce_fusion.6
  137.3 4.6 %all-to-all-start.3 = ((f32[8,1,128]{2,1,0:T(1,128)}), f32[8,1,128]{2,1,0:T(1,128)S(1)}, u32[]{:S(2)}, u32[]{:S(2)}) async-start(f32[8,1,128]{2,1,0:T(1,128)} %reshape.252), calls=%async_computation.3 | async-start | bytes 8192 | tf_op jit(solution)/shard_map/all_to_all | solution.py:177
  143.1 5.2 %all-to-all-done.3 = f32[8,1,128]{2,1,0:T(1,128)S(1)} async-done(((f32[8,1,128]{2,1,0:T(1,128)}), f32[8,1,128]{2,1,0:T(1,128)S(1)}, u32[]{:S(2)}, u32[]{:S(2)}) %all-to-all-start.3) | async-done | bytes 4128 | tf_op jit(solution)/shard_map/all_to_all | solution.py:177
  148.3 3.3 %all-to-all-start.2 = ((f32[8,1,128]{2,1,0:T(1,128)}), f32[8,1,128]{2,1,0:T(1,128)S(1)}, u32[]{:S(2)}, u32[]{:S(2)}) async-start(f32[8,1,128]{2,1,0:T(1,128)} %reshape.250), calls=%async_computation.2 | async-start | bytes 8192 | tf_op jit(solution)/shard_map/all_to_all | solution.py:177
  153.2 4.7 %all-to-all-done.2 = f32[8,1,128]{2,1,0:T(1,128)S(1)} async-done(((f32[8,1,128]{2,1,0:T(1,128)}), f32[8,1,128]{2,1,0:T(1,128)S(1)}, u32[]{:S(2)}, u32[]{:S(2)}) %all-to-all-start.2) | async-done | bytes 4128 | tf_op jit(solution)/shard_map/all_to_all | solution.py:177
  162.5 3.3 %all-to-all-start.5 = ((f32[8,1,128]{2,1,0:T(1,128)}), f32[8,1,128]{2,1,0:T(1,128)S(1)}, u32[]{:S(2)}, u32[]{:S(2)}) async-start(f32[8,1,128]{2,1,0:T(1,128)} %reshape.256), calls=%async_computation.5 | async-start | bytes 8192 | tf_op jit(solution)/shard_map/all_to_all | solution.py:177
  166.7 5.5 %all-to-all-done.5 = f32[8,1,128]{2,1,0:T(1,128)S(1)} async-done(((f32[8,1,128]{2,1,0:T(1,128)}), f32[8,1,128]{2,1,0:T(1,128)S(1)}, u32[]{:S(2)}, u32[]{:S(2)}) %all-to-all-start.5) | async-done | bytes 4128 | tf_op jit(solution)/shard_map/all_to_all | solution.py:177
  172.2 3.3 %all-to-all-start.4 = ((f32[8,1,128]{2,1,0:T(1,128)}), f32[8,1,128]{2,1,0:T(1,128)S(1)}, u32[]{:S(2)}, u32[]{:S(2)}) async-start(f32[8,1,128]{2,1,0:T(1,128)} %reshape.254), calls=%async_computation.4 | async-start | bytes 8192 | tf_op jit(solution)/shard_map/all_to_all | solution.py:177
  176.5 5.3 %all-to-all-done.4 = f32[8,1,128]{2,1,0:T(1,128)S(1)} async-done(((f32[8,1,128]{2,1,0:T(1,128)}), f32[8,1,128]{2,1,0:T(1,128)S(1)}, u32[]{:S(2)}, u32[]{:S(2)}) %all-to-all-start.4) | async-done | bytes 4128 | tf_op jit(solution)/shard_map/all_to_all | solution.py:177
  184.9 5.3 %all_gather.14 = bf16[64,544]{1,0:T(8,128)(2,1)S(1)} all-gather(bf16[16,544]{1,0:T(8,128)(2,1)S(1)} %get-tuple-element.76), channel_id=1, replica_groups=mesh['rows'=8,'scen'=4] {'scen'}, dimensions={0}, use_global_device_ids=true | all-gather | bytes 87040 | tf_op jit(solution)/shard_map/all_gather | solution.py:180
  190.6 6.1 %all-reduce.1 = f32[64]{0:T(128)S(1)} all-reduce(f32[64]{0:T(128)S(1)} %dynamic-update-slice), channel_id=1, replica_groups=mesh['rows'=8,'scen'=4] {'scen'}, use_global_device_ids=true, to_apply=%add.1 | all-reduce | flops 64 | bytes 512
  196.7 4.3 %convolution_subtract_fusion = f32[64,2048]{1,0:T(8,128)} fusion(bf16[1024,2048]{1,0:T(8,128)(2,1)} %param.15, bf16[64,544]{1,0:T(8,128)(2,1)S(1)} %all_gather.14, s32[1024]{0:T(1024)S(1)} %iota_add_fusion.1, s32[544]{0:T(1024)S(1)} %select_n.202, f32[64,2048]{1,0:T(8,128)S(1)} %get-tuple-element.65, f32[64]{0:T(128)S(1)} %all-reduce.1), kind=kOutput, calls=%fused_computation.7 | convolution fusion | flops 340623360 | bytes 5319040 | tf_op jit(solution)/shard_map/dot_general | solution.py:183
  201.3 8.9 %all_to_all.42 = f32[8,1,512]{2,1,0:T(1,128)S(1)} all-to-all(f32[8,1,512]{2,1,0:T(1,128)S(1)} %reshape.258), channel_id=1, replica_groups=mesh['rows'=8,'scen'=4] {'rows'}, dimensions={0} | all-to-all | bytes 32768 | tf_op jit(solution)/shard_map/all_to_all | solution.py:186
  212.0 8.1 %reduce-scatter.2.cloned.1.call-done = f32[16,2048]{1,0:T(8,128)} async-done(((f32[64,2048]{1,0:T(8,128)}), f32[16,2048]{1,0:T(8,128)}) %reduce-scatter.2.cloned.1.call-update) | async-done | bytes 131088 | tf_op jit(solution)/shard_map/reduce_scatter | solution.py:184
  (194 shorter events, 38.4 us)
Async XLA Ops:
  7.2 48.7 %copy-start = (f32[16,2048]{1,0:T(8,128)S(1)}, f32[16,2048]{1,0:T(8,128)}, u32[]{:S(2)}) copy-start(f32[16,2048]{1,0:T(8,128)} %param.16) | copy-start | bytes 393220
  8.8 33.1 %copy-start.4 = (s32[128]{0:T(128)}, s32[128]{0:T(128)S(1)}, u32[]{:S(2)}) copy-start(s32[128]{0:T(128)S(1)} %fusion.143) | copy-start | bytes 1540
  11.1 32.9 %all-to-all-start.1 = ((f32[8,1,80]{2,1,0:T(1,128)}), f32[8,1,80]{2,1,0:T(1,128)S(1)}, u32[]{:S(2)}, u32[]{:S(2)}) async-start(f32[8,1,80]{2,1,0:T(1,128)} %bitcast.19), calls=%async_computation.1 | async-start | bytes 8192 | tf_op jit(solution)/shard_map/all_to_all | solution.py:73
  20.8 39.7 %collective-permute-start.1 = (f32[130,16]{0,1:T(8,128)S(1)}, f32[130,16]{0,1:T(8,128)S(1)}, u32[]{:S(2)}, u32[]{:S(2)}) collective-permute-start(f32[130,16]{0,1:T(8,128)S(1)} %pad_maximum_fusion.14), channel_id=1, source_target_pairs={{0,4},{4,0},{8,12},{12,8},{16,20},{20,16},{24,28},{28,24},{1,5},{5... | collective-permute-start | bytes 24968 | tf_op jit(solution)/shard_map/ppermute | solution.py:10
  38.7 4.1 %copy-start.6 = (u32[32]{0:T(128)S(1)}, u32[32]{0:T(128)}, u32[]{:S(2)}) copy-start(u32[32]{0:T(128)} %constant.102) | copy-start | bytes 388
  44.8 84.1 %all-to-all-start = ((f32[8,114,64]{1,2,0:T(8,128)}), f32[8,114,64]{1,2,0:T(8,128)S(1)}, u32[]{:S(2)}, u32[]{:S(2)}) async-start(f32[8,114,64]{1,2,0:T(8,128)} %bitcast.8), calls=%async_computation | async-start | bytes 524288 | tf_op jit(solution)/shard_map/all_to_all | solution.py:95
  49.3 41.4 %all-reduce.5.cloned.1.call-start = ((), (), s32[]{:S(2)}) async-start(), calls=%async_computation.8 | async-start | bytes 696320 | tf_op jit(solution)/shard_map/psum | solution.py:119
  56.9 68.2 %all-reduce.7.cloned.1.call-start = ((), (), s32[]{:S(2)}) async-start(), calls=%async_computation.9 | async-start | bytes 196608 | tf_op jit(solution)/shard_map/psum | solution.py:123
  57.7 74.1 %collective-permute-start = (f32[16,272]{1,0:T(8,128)S(1)}, f32[16,272]{1,0:T(8,128)S(1)}, u32[]{:S(2)}, u32[]{:S(2)}) collective-permute-start(f32[16,272]{1,0:T(8,128)S(1)} %fusion.39), channel_id=1, source_target_pairs={{0,4},{4,0},{8,12},{12,8},{16,20},{20,16},{24,28},{28,24},{1,5},{5... | collective-permute-start | bytes 52232 | tf_op jit(solution)/shard_map/ppermute | solution.py:10
  90.7 37.8 %copy-start.1 = (bf16[544,272]{0,1:T(8,128)(2,1)S(1)}, bf16[544,272]{0,1:T(8,128)(2,1)}, u32[]{:S(2)}) copy-start(bf16[544,272]{0,1:T(8,128)(2,1)} %all-reduce.5.cloned.1.call-done) | copy-start | bytes 887812
  92.0 36.2 %collective-permute-start.2 = (bf16[272,272]{0,1:T(8,128)(2,1)S(1)}, bf16[272,272]{0,1:T(8,128)(2,1)S(1)}, u32[]{:S(2)}, u32[]{:S(2)}) collective-permute-start(bf16[272,272]{0,1:T(8,128)(2,1)S(1)} %get-tuple-element.22), channel_id=1, source_target_pairs={{0,4},{4,0},{8,12},{12,8},{16,20},{20,16},{24,28},{28,24},{1,5},{5... | collective-permute-start | bytes 443912 | tf_op jit(solution)/shard_map/ppermute | solution.py:10
  125.9 6.0 %collective-permute-start.3 = (f32[16,273]{1,0:T(8,128)S(1)}, f32[16,273]{1,0:T(8,128)}, u32[]{:S(2)}, u32[]{:S(2)}) collective-permute-start(f32[16,273]{1,0:T(8,128)S(1)} %constant_dynamic-slice_fusion), channel_id=1, source_target_pairs={{0,4},{4,0},{8,12},{12,8},{16,20},{20,16},{24,28},{28,24},{1,5},{5... | collective-permute-start | bytes 52424 | tf_op jit(solution)/shard_map/ppermute | solution.py:10
  131.3 3.9 %copy-start.2 = (f32[16,16]{1,0:T(8,128)S(1)}, f32[16,16]{1,0:T(8,128)}, u32[]{:S(2)}) copy-start(f32[16,16]{1,0:T(8,128)} %get-tuple-element.59) | copy-start | bytes 3076
  131.3 3.9 %copy-start.3 = (pred[544]{0:T(1024)(128)(4,1)S(1)}, pred[544]{0:T(1024)(128)(4,1)}, u32[]{:S(2)}) copy-start(pred[544]{0:T(1024)(128)(4,1)} %broadcast_compare_fusion) | copy-start | bytes 1636
  137.3 11.0 %all-to-all-start.3 = ((f32[8,1,128]{2,1,0:T(1,128)}), f32[8,1,128]{2,1,0:T(1,128)S(1)}, u32[]{:S(2)}, u32[]{:S(2)}) async-start(f32[8,1,128]{2,1,0:T(1,128)} %reshape.252), calls=%async_computation.3 | async-start | bytes 8192 | tf_op jit(solution)/shard_map/all_to_all | solution.py:177
  148.3 9.6 %all-to-all-start.2 = ((f32[8,1,128]{2,1,0:T(1,128)}), f32[8,1,128]{2,1,0:T(1,128)S(1)}, u32[]{:S(2)}, u32[]{:S(2)}) async-start(f32[8,1,128]{2,1,0:T(1,128)} %reshape.250), calls=%async_computation.2 | async-start | bytes 8192 | tf_op jit(solution)/shard_map/all_to_all | solution.py:177
  162.5 9.6 %all-to-all-start.5 = ((f32[8,1,128]{2,1,0:T(1,128)}), f32[8,1,128]{2,1,0:T(1,128)S(1)}, u32[]{:S(2)}, u32[]{:S(2)}) async-start(f32[8,1,128]{2,1,0:T(1,128)} %reshape.256), calls=%async_computation.5 | async-start | bytes 8192 | tf_op jit(solution)/shard_map/all_to_all | solution.py:177
  172.2 9.6 %all-to-all-start.4 = ((f32[8,1,128]{2,1,0:T(1,128)}), f32[8,1,128]{2,1,0:T(1,128)S(1)}, u32[]{:S(2)}, u32[]{:S(2)}) async-start(f32[8,1,128]{2,1,0:T(1,128)} %reshape.254), calls=%async_computation.4 | async-start | bytes 8192 | tf_op jit(solution)/shard_map/all_to_all | solution.py:177
  175.5 44.6 %reduce-scatter.2.cloned.1.call-start = ((), (), s32[]{:S(2)}) async-start(), calls=%async_computation.10 | async-start | bytes 655360 | tf_op jit(solution)/shard_map/reduce_scatter | solution.py:184
  196.7 14.5 %copy-start.5 = (s32[128]{0:T(128)S(1)}, s32[128]{0:T(128)}, u32[]{:S(2)}) copy-start(s32[128]{0:T(128)} %copy-done.4) | copy-start | bytes 1540
Sparse Core Ops, SparseCore 0:
  57.1 33.6 all-reduce.4
  93.6 31.4 all-reduce.6
  201.1 18.9 reduce-scatter.1
where the time goes:
time: 228 us; the launch traced here: 227 us
  waiting for transfers between devices  88.3 us (39%)
  starting transfers between devices  33.7 us (15%)
  blocking collectives  30.7 us (13%)
  matrix products  24.3 us (11%)
  local copies, waits for them, and re-layouts  21.1 us (9%)
  between operations  15 us (7%)
  other arithmetic  13.6 us (6%)
    psum x1, waiting for transfers between devices, per_device(): side = lax.psum(jnp.concatenate([pts_part, depth_part], 1), 'scen')  31.6 us
    psum x1, waiting for transfers between devices, per_device(): own_cols = lax.psum(part, 'scen')  27.9 us
    all_to_all x4, waiting for transfers between devices, per_device(): lax.all_to_all(out.reshape(n, 2, scen, 2 * ends // n), 'rows', 0, 0, tile...  20.7 us
    all_to_all x4, starting transfers between devices, per_device(): lax.all_to_all(out.reshape(n, 2, scen, 2 * ends // n), 'rows', 0, 0, tile...  14.5 us
    all_to_all x1, blocking collectives, per_device(): lax.all_to_all(own_current.reshape(scen, n, slots).transpose(1, 0, 2), 'r...  8.94 us
    dot_general x9, matrix products, exact_dot(): return jnp.dot(left, right, precision=lax.Precision.HIGHEST)  8.49 us
    reduce_scatter x1, waiting for transfers between devices, per_device(): voltage = lax.psum_scatter(partial, 'scen', scatter_dimension=0, tiled=True)  8.07 us
    all_to_all x1, starting transfers between devices, per_device(): lax.all_to_all(jnp.concatenate([bus_out, ends_out], 1), 'rows', 0, 0, til...  7.28 us
  transfers between devices with their start and end apart: 13, of which 7 were waited for; matrix products, arithmetic and copies ran while one was open for 17% of the time, Pallas kernels for 0%

commit v1 on v0

--- a/solution.py
+++ b/solution.py
@@ -120,7 +120,7 @@
     branch_part = jnp.dot(picks, inverse, preferred_element_type=f32)
     pts_part = jnp.dot(picks, narrow, preferred_element_type=f32)
     depth_part = jnp.sum(branch_part * col_picks, axis=1, keepdims=True)
-    side = lax.psum(jnp.concatenate([pts_part, depth_part], 1), "scen")
+    side = jnp.sum(lax.all_gather(jnp.concatenate([pts_part, depth_part], 1), "scen"), axis=0)
     side = lax.dynamic_slice_in_dim(side, share * scen, scen, axis=0)
     own_diag = lax.dynamic_slice_in_dim(own_cols, half * hp, hp, axis=0)
     cross = lax.dynamic_slice_in_dim(own_cols, (1 - half) * hp, hp, axis=0).T

time: 228 us -> 211 us (0.925)
  waiting for transfers between devices: 88.3 us -> 63.4 us
  blocking collectives: 30.7 us -> 37.9 us
    psum x1 -> x0, waiting for transfers between devices: 31.6 us -> none  [per_device(): side = lax.psum(jnp.concatenate([pts_part, depth_part], 1), 'scen')]
    all_gather x0 -> x1, blocking collectives: none -> 6.63 us  [per_device(): lax.all_gather(jnp.concatenate([pts_part, depth_part], 1), 'scen')]
    psum x1, waiting for transfers between devices: 27.9 us -> 31.7 us  [per_device(): own_cols = lax.psum(part, 'scen')]
    ppermute x4, waiting for transfers between devices: 0.01 us -> 3.51 us  [swapped(): return lax.ppermute(value, axis, pairs)]
  transfers between devices with their start and end apart: 13 -> 12, of which waited for: 7 -> 7; matrix products, arithmetic and copies ran while one was open for 17% -> 18% of each run, Pallas kernels for 0% -> 0%
where the time goes in v1:
time: 211 us; the launch traced here: 209 us
  waiting for transfers between devices  63.4 us (30%)
  blocking collectives  37.9 us (18%)
  starting transfers between devices  33.2 us (16%)
  matrix products  24.9 us (12%)
  local copies, waits for them, and re-layouts  20.9 us (10%)
  between operations  15.3 us (7%)
  other arithmetic  13.8 us (7%)
    psum x1, waiting for transfers between devices, per_device(): own_cols = lax.psum(part, 'scen')  31.7 us
    all_to_all x4, waiting for transfers between devices, per_device(): lax.all_to_all(out.reshape(n, 2, scen, 2 * ends // n), 'rows', 0, 0, tile...  20.7 us
    all_to_all x4, starting transfers between devices, per_device(): lax.all_to_all(out.reshape(n, 2, scen, 2 * ends // n), 'rows', 0, 0, tile...  15.7 us
    dot_general x9, matrix products, exact_dot(): return jnp.dot(left, right, precision=lax.Precision.HIGHEST)  9.12 us
    all_to_all x1, blocking collectives, per_device(): lax.all_to_all(own_current.reshape(scen, n, slots).transpose(1, 0, 2), 'r...  8.94 us
    reduce_scatter x1, waiting for transfers between devices, per_device(): voltage = lax.psum_scatter(partial, 'scen', scatter_dimension=0, tiled=True)  7.48 us
    all_to_all x1, starting transfers between devices, per_device(): lax.all_to_all(jnp.concatenate([bus_out, ends_out], 1), 'rows', 0, 0, til...  7.28 us
    unnamed x1, blocking collectives  6.67 us
  transfers between devices with their start and end apart: 12, of which 7 were waited for; matrix products, arithmetic and copies ran while one was open for 18% of the time, Pallas kernels for 0%

profile of v1, /device:TPU:0, one launch (start us, length us, event | category | flops | bytes accessed | tf_op | source)
XLA Modules:
  0.0 209.4 jit_solution(11268933911044145062)
XLA Ops:
  11.1 7.3 %all-to-all-start.1 = ((f32[8,1,80]{2,1,0:T(1,128)}), f32[8,1,80]{2,1,0:T(1,128)S(1)}, u32[]{:S(2)}, u32[]{:S(2)}) async-start(f32[8,1,80]{2,1,0:T(1,128)} %bitcast.19), calls=%async_computation.1 | async-start | bytes 8192 | tf_op jit(solution)/shard_map/all_to_all | solution.py:73
  20.8 2.0 collective-permute-start.1
  23.7 5.2 %all-gather.1 = s32[1,64,4]{2,0,1:T(1,128)S(1)} all-gather(s32[1,16,4]{2,0,1:T(1,128)S(1)} %copy.320), channel_id=3, replica_groups=mesh['rows'=8,'scen'=4] {'scen'}, dimensions={1}, use_global_device_ids=true | all-gather | bytes 1280 | tf_op jit(solution)/shard_map/all_gather | solution.py:106
  29.0 5.2 %all-gather = s32[1,64,4]{2,0,1:T(1,128)S(1)} all-gather(s32[1,16,4]{2,0,1:T(1,128)S(1)} %copy.319), channel_id=2, replica_groups=mesh['rows'=8,'scen'=4] {'scen'}, dimensions={1}, use_global_device_ids=true | all-gather | bytes 1280 | tf_op jit(solution)/shard_map/all_gather | solution.py:103
  34.2 1.3 dynamic-slice_reduce_fusion
  35.5 1.3 dynamic-slice_reduce_fusion.1
  38.7 3.2 %multiply_reduce_fusion = (f32[64]{0:T(128)S(1)}, f32[64,2048]{1,0:T(8,128)S(1)}) fusion(s32[2048]{0:T(1024)S(1)} %iota_add_fusion, s32[64]{0:T(128)S(1)} %dynamic-slice_reduce_fusion, s32[64]{0:T(128)S(1)} %dynamic-slice_reduce_fusion.1, bf16[1024,2048]{1,0:T(8,128)(2,1)} %param.15, s32[1024]{0:T(1024)S(1)} %iota_add_fusion.1), kind=kOutput, calls=%fused_computation.54 | convolution fusion | flops 269680576 | bytes 4731648 | tf_op jit(solution)/shard_map/dot_general | solution.py:120
  44.8 4.5 %all-to-all-start = ((f32[8,114,64]{1,2,0:T(8,128)}), f32[8,114,64]{1,2,0:T(8,128)S(1)}, u32[]{:S(2)}, u32[]{:S(2)}) async-start(f32[8,114,64]{1,2,0:T(8,128)} %bitcast.8), calls=%async_computation | async-start | bytes 524288 | tf_op jit(solution)/shard_map/all_to_all | solution.py:95
  49.7 4.1 %fusion.16 = bf16[272,1024]{1,0:T(8,128)(2,1)S(1)} fusion(bf16[1024,2048]{1,0:T(8,128)(2,1)} %param.15, s32[272]{0:T(512)S(1)} %fusion.142), kind=kOutput, calls=%fused_computation.21 | convolution fusion | flops 1142243328 | bytes 4752448 | tf_op jit(solution)/shard_map/dot_general | solution.py:117
  54.2 6.6 %all-gather.2 = f32[256,273]{1,0:T(8,128)S(1)} all-gather(f32[64,273]{1,0:T(8,128)S(1)} %pad_maximum_fusion.12), channel_id=4, replica_groups=mesh['rows'=8,'scen'=4] {'scen'}, dimensions={0}, use_global_device_ids=true | all-gather | bytes 349440 | tf_op jit(solution)/shard_map/all_gather | solution.py:123
  62.4 1.5 fusion.19
  63.8 2.0 collective-permute-start.3
  66.4 1.6 fusion.39
  69.8 31.7 %all-reduce.4.cloned.1.call-done = bf16[544,272]{0,1:T(8,128)(2,1)} async-done(((bf16[544,272]{0,1:T(8,128)(2,1)}), bf16[544,272]{0,1:T(8,128)(2,1)}) %all-reduce.4.cloned.1.call-update) | async-done | bytes 295952 | tf_op jit(solution)/shard_map/psum | solution.py:119
  101.5 1.3 constant_dynamic-slice_fusion.4
  102.9 1.5 collective-permute-start.2
  105.2 3.5 %collective-permute-done.2 = bf16[272,272]{0,1:T(8,128)(2,1)S(1)} collective-permute-done((bf16[272,272]{0,1:T(8,128)(2,1)S(1)}, bf16[272,272]{0,1:T(8,128)(2,1)S(1)}, u32[]{:S(2)}, u32[]{:S(2)}) %collective-permute-start.2) | collective-permute-done | bytes 148000 | tf_op jit(solution)/shard_map/ppermute | solution.py:10
  109.3 1.2 pad_slice_fusion.1
  113.2 1.6 multiply_reduce_fusion.6
  118.6 5.8 %all-to-all-start.3 = ((f32[8,1,128]{2,1,0:T(1,128)}), f32[8,1,128]{2,1,0:T(1,128)S(1)}, u32[]{:S(2)}, u32[]{:S(2)}) async-start(f32[8,1,128]{2,1,0:T(1,128)} %reshape.253), calls=%async_computation.3 | async-start | bytes 8192 | tf_op jit(solution)/shard_map/all_to_all | solution.py:177
  125.5 5.2 %all-to-all-done.3 = f32[8,1,128]{2,1,0:T(1,128)S(1)} async-done(((f32[8,1,128]{2,1,0:T(1,128)}), f32[8,1,128]{2,1,0:T(1,128)S(1)}, u32[]{:S(2)}, u32[]{:S(2)}) %all-to-all-start.3) | async-done | bytes 4128 | tf_op jit(solution)/shard_map/all_to_all | solution.py:177
  130.8 3.3 %all-to-all-start.2 = ((f32[8,1,128]{2,1,0:T(1,128)}), f32[8,1,128]{2,1,0:T(1,128)S(1)}, u32[]{:S(2)}, u32[]{:S(2)}) async-start(f32[8,1,128]{2,1,0:T(1,128)} %reshape.251), calls=%async_computation.2 | async-start | bytes 8192 | tf_op jit(solution)/shard_map/all_to_all | solution.py:177
  135.7 4.7 %all-to-all-done.2 = f32[8,1,128]{2,1,0:T(1,128)S(1)} async-done(((f32[8,1,128]{2,1,0:T(1,128)}), f32[8,1,128]{2,1,0:T(1,128)S(1)}, u32[]{:S(2)}, u32[]{:S(2)}) %all-to-all-start.2) | async-done | bytes 4128 | tf_op jit(solution)/shard_map/all_to_all | solution.py:177
  145.0 3.3 %all-to-all-start.5 = ((f32[8,1,128]{2,1,0:T(1,128)}), f32[8,1,128]{2,1,0:T(1,128)S(1)}, u32[]{:S(2)}, u32[]{:S(2)}) async-start(f32[8,1,128]{2,1,0:T(1,128)} %reshape.257), calls=%async_computation.5 | async-start | bytes 8192 | tf_op jit(solution)/shard_map/all_to_all | solution.py:177
  149.1 5.5 %all-to-all-done.5 = f32[8,1,128]{2,1,0:T(1,128)S(1)} async-done(((f32[8,1,128]{2,1,0:T(1,128)}), f32[8,1,128]{2,1,0:T(1,128)S(1)}, u32[]{:S(2)}, u32[]{:S(2)}) %all-to-all-start.5) | async-done | bytes 4128 | tf_op jit(solution)/shard_map/all_to_all | solution.py:177
  154.6 3.3 %all-to-all-start.4 = ((f32[8,1,128]{2,1,0:T(1,128)}), f32[8,1,128]{2,1,0:T(1,128)S(1)}, u32[]{:S(2)}, u32[]{:S(2)}) async-start(f32[8,1,128]{2,1,0:T(1,128)} %reshape.255), calls=%async_computation.4 | async-start | bytes 8192 | tf_op jit(solution)/shard_map/all_to_all | solution.py:177
  159.0 5.3 %all-to-all-done.4 = f32[8,1,128]{2,1,0:T(1,128)S(1)} async-done(((f32[8,1,128]{2,1,0:T(1,128)}), f32[8,1,128]{2,1,0:T(1,128)S(1)}, u32[]{:S(2)}, u32[]{:S(2)}) %all-to-all-start.4) | async-done | bytes 4128 | tf_op jit(solution)/shard_map/all_to_all | solution.py:177
  167.3 5.3 %all_gather.22 = bf16[64,544]{1,0:T(8,128)(2,1)S(1)} all-gather(bf16[16,544]{1,0:T(8,128)(2,1)S(1)} %get-tuple-element.76), channel_id=1, replica_groups=mesh['rows'=8,'scen'=4] {'scen'}, dimensions={0}, use_global_device_ids=true | all-gather | bytes 87040 | tf_op jit(solution)/shard_map/all_gather | solution.py:180
  173.1 6.7 %all-reduce.1 = f32[64]{0:T(128)S(1)} all-reduce(f32[64]{0:T(128)S(1)} %dynamic-update-slice), channel_id=1, replica_groups=mesh['rows'=8,'scen'=4] {'scen'}, use_global_device_ids=true, to_apply=%add.1 | all-reduce | flops 64 | bytes 512
  179.7 4.3 %convolution_subtract_fusion = f32[64,2048]{1,0:T(8,128)} fusion(bf16[1024,2048]{1,0:T(8,128)(2,1)} %param.15, bf16[64,544]{1,0:T(8,128)(2,1)S(1)} %all_gather.22, s32[1024]{0:T(1024)S(1)} %iota_add_fusion.1, s32[544]{0:T(1024)S(1)} %select_n.202, f32[64,2048]{1,0:T(8,128)S(1)} %get-tuple-element.65, f32[64]{0:T(128)S(1)} %all-reduce.1), kind=kOutput, calls=%fused_computation.7 | convolution fusion | flops 340623360 | bytes 5319040 | tf_op jit(solution)/shard_map/dot_general | solution.py:183
  184.3 8.9 %all_to_all.42 = f32[8,1,512]{2,1,0:T(1,128)S(1)} all-to-all(f32[8,1,512]{2,1,0:T(1,128)S(1)} %reshape.259), channel_id=1, replica_groups=mesh['rows'=8,'scen'=4] {'rows'}, dimensions={0} | all-to-all | bytes 32768 | tf_op jit(solution)/shard_map/all_to_all | solution.py:186
  195.1 7.5 %reduce-scatter.2.cloned.1.call-done = f32[16,2048]{1,0:T(8,128)} async-done(((f32[64,2048]{1,0:T(8,128)}), f32[16,2048]{1,0:T(8,128)}) %reduce-scatter.2.cloned.1.call-update) | async-done | bytes 131088 | tf_op jit(solution)/shard_map/reduce_scatter | solution.py:184
  (193 shorter events, 38.3 us)
Async XLA Ops:
  7.2 59.2 %copy-start = (f32[16,2048]{1,0:T(8,128)S(1)}, f32[16,2048]{1,0:T(8,128)}, u32[]{:S(2)}) copy-start(f32[16,2048]{1,0:T(8,128)} %param.16) | copy-start | bytes 393220
  8.8 33.1 %copy-start.4 = (s32[128]{0:T(128)}, s32[128]{0:T(128)S(1)}, u32[]{:S(2)}) copy-start(s32[128]{0:T(128)S(1)} %fusion.143) | copy-start | bytes 1540
  11.1 32.9 %all-to-all-start.1 = ((f32[8,1,80]{2,1,0:T(1,128)}), f32[8,1,80]{2,1,0:T(1,128)S(1)}, u32[]{:S(2)}, u32[]{:S(2)}) async-start(f32[8,1,80]{2,1,0:T(1,128)} %bitcast.19), calls=%async_computation.1 | async-start | bytes 8192 | tf_op jit(solution)/shard_map/all_to_all | solution.py:73
  20.8 47.3 %collective-permute-start.1 = (f32[130,16]{0,1:T(8,128)S(1)}, f32[130,16]{0,1:T(8,128)S(1)}, u32[]{:S(2)}, u32[]{:S(2)}) collective-permute-start(f32[130,16]{0,1:T(8,128)S(1)} %pad_maximum_fusion.14), channel_id=1, source_target_pairs={{0,4},{4,0},{8,12},{12,8},{16,20},{20,16},{24,28},{28,24},{1,5},{5... | collective-permute-start | bytes 24968 | tf_op jit(solution)/shard_map/ppermute | solution.py:10
  38.7 4.1 %copy-start.6 = (u32[32]{0:T(128)S(1)}, u32[32]{0:T(128)}, u32[]{:S(2)}) copy-start(u32[32]{0:T(128)} %constant.102) | copy-start | bytes 388
  44.8 64.5 %all-to-all-start = ((f32[8,114,64]{1,2,0:T(8,128)}), f32[8,114,64]{1,2,0:T(8,128)S(1)}, u32[]{:S(2)}, u32[]{:S(2)}) async-start(f32[8,114,64]{1,2,0:T(8,128)} %bitcast.8), calls=%async_computation | async-start | bytes 524288 | tf_op jit(solution)/shard_map/all_to_all | solution.py:95
  49.3 52.2 %all-reduce.4.cloned.1.call-start = ((), (), s32[]{:S(2)}) async-start(), calls=%async_computation.8 | async-start | bytes 696320 | tf_op jit(solution)/shard_map/psum | solution.py:119
  63.8 49.3 %collective-permute-start.3 = (f32[16,273]{1,0:T(8,128)}, f32[16,273]{1,0:T(8,128)}, u32[]{:S(2)}, u32[]{:S(2)}) collective-permute-start(f32[16,273]{1,0:T(8,128)} %constant_dynamic-slice_fusion), channel_id=1, source_target_pairs={{0,4},{4,0},{8,12},{12,8},{16,20},{20,16},{24,28},{28,24},{1,5},{5... | collective-permute-start | bytes 52424 | tf_op jit(solution)/shard_map/ppermute | solution.py:10
  68.0 44.2 %collective-permute-start = (f32[16,272]{1,0:T(8,128)}, f32[16,272]{1,0:T(8,128)}, u32[]{:S(2)}, u32[]{:S(2)}) collective-permute-start(f32[16,272]{1,0:T(8,128)} %fusion.39), channel_id=1, source_target_pairs={{0,4},{4,0},{8,12},{12,8},{16,20},{20,16},{24,28},{28,24},{1,5},{5... | collective-permute-start | bytes 52232 | tf_op jit(solution)/shard_map/ppermute | solution.py:10
  101.5 7.4 %copy-start.1 = (bf16[544,272]{0,1:T(8,128)(2,1)S(1)}, bf16[544,272]{0,1:T(8,128)(2,1)}, u32[]{:S(2)}) copy-start(bf16[544,272]{0,1:T(8,128)(2,1)} %all-reduce.4.cloned.1.call-done) | copy-start | bytes 887812
  102.9 5.9 %collective-permute-start.2 = (bf16[272,272]{0,1:T(8,128)(2,1)S(1)}, bf16[272,272]{0,1:T(8,128)(2,1)S(1)}, u32[]{:S(2)}, u32[]{:S(2)}) collective-permute-start(bf16[272,272]{0,1:T(8,128)(2,1)S(1)} %get-tuple-element.22), channel_id=1, source_target_pairs={{0,4},{4,0},{8,12},{12,8},{16,20},{20,16},{24,28},{28,24},{1,5},{5... | collective-permute-start | bytes 443912 | tf_op jit(solution)/shard_map/ppermute | solution.py:10
  111.7 4.7 %copy-start.2 = (f32[16,16]{1,0:T(8,128)S(1)}, f32[16,16]{1,0:T(8,128)}, u32[]{:S(2)}) copy-start(f32[16,16]{1,0:T(8,128)} %get-tuple-element.59) | copy-start | bytes 3076
  111.7 4.7 %copy-start.3 = (pred[544]{0:T(1024)(128)(4,1)S(1)}, pred[544]{0:T(1024)(128)(4,1)}, u32[]{:S(2)}) copy-start(pred[544]{0:T(1024)(128)(4,1)} %broadcast_compare_fusion) | copy-start | bytes 1636
  118.6 12.2 %all-to-all-start.3 = ((f32[8,1,128]{2,1,0:T(1,128)}), f32[8,1,128]{2,1,0:T(1,128)S(1)}, u32[]{:S(2)}, u32[]{:S(2)}) async-start(f32[8,1,128]{2,1,0:T(1,128)} %reshape.253), calls=%async_computation.3 | async-start | bytes 8192 | tf_op jit(solution)/shard_map/all_to_all | solution.py:177
  130.8 9.6 %all-to-all-start.2 = ((f32[8,1,128]{2,1,0:T(1,128)}), f32[8,1,128]{2,1,0:T(1,128)S(1)}, u32[]{:S(2)}, u32[]{:S(2)}) async-start(f32[8,1,128]{2,1,0:T(1,128)} %reshape.251), calls=%async_computation.2 | async-start | bytes 8192 | tf_op jit(solution)/shard_map/all_to_all | solution.py:177
  145.0 9.6 %all-to-all-start.5 = ((f32[8,1,128]{2,1,0:T(1,128)}), f32[8,1,128]{2,1,0:T(1,128)S(1)}, u32[]{:S(2)}, u32[]{:S(2)}) async-start(f32[8,1,128]{2,1,0:T(1,128)} %reshape.257), calls=%async_computation.5 | async-start | bytes 8192 | tf_op jit(solution)/shard_map/all_to_all | solution.py:177
  154.6 9.6 %all-to-all-start.4 = ((f32[8,1,128]{2,1,0:T(1,128)}), f32[8,1,128]{2,1,0:T(1,128)S(1)}, u32[]{:S(2)}, u32[]{:S(2)}) async-start(f32[8,1,128]{2,1,0:T(1,128)} %reshape.255), calls=%async_computation.4 | async-start | bytes 8192 | tf_op jit(solution)/shard_map/all_to_all | solution.py:177
  157.9 44.6 %reduce-scatter.2.cloned.1.call-start = ((), (), s32[]{:S(2)}) async-start(), calls=%async_computation.9 | async-start | bytes 655360 | tf_op jit(solution)/shard_map/reduce_scatter | solution.py:184
  179.7 14.5 %copy-start.5 = (s32[128]{0:T(128)S(1)}, s32[128]{0:T(128)}, u32[]{:S(2)}) copy-start(s32[128]{0:T(128)} %copy-done.4) | copy-start | bytes 1540
Sparse Core Ops, SparseCore 0:
  68.2 33.2 all-reduce.3
  184.2 18.3 reduce-scatter.1
